TPU v7x, 32 devices: a whole 2x2x4 slice. The times are simulated.
32 devices in a mesh: mem: 8 (over y, x, core), st: 4 (over z).
Axes of the slice: x: 2, y: 2, z: 4, core: 2. Of those that a mesh axis runs over, the one named last changes fastest.
Arguments:
- ensemble: float32 [8192, 256], P('st', 'mem'), may hold values from -8 to 8
- obs_values: float32 [4, 8, 128], replicated, may hold values from -8 to 8
- obs_sigma: float32 [4, 8, 128], replicated, may hold values from 0.25 to 0.5
- obs_operator: float32 [4, 8, 2, 128, 128], replicated, may hold values from -0.375 to 0.375
- block_cols: int32 [4, 8, 2], replicated, may hold values from 0 to 63
- batch_order: int32 [4], replicated, may hold values from 0 to 3, each once
Outputs:
- analysis: float32 [8192, 256], P('st', 'mem')
- log_weights: float32 [256], P('mem')
- ess: float32 [], replicated
Inputs may be any that keep to these rules, and one draw needn't show every extreme that they name: `block_cols`: block indices of the whole state. `batch_order`: each batch exactly once.
All inputs are finite; a program needn't handle non-finite values.
Results may differ from a plain program's by a relative error of at most 0.0003.
Values sent between devices are 32-bit elements; how exact they have to be, the bound alone decides.
A program may use at most 64 MiB of HBM per device.

v0:
```python
import math
import jax
import jax.numpy as jnp
from jax import lax
from jax.sharding import PartitionSpec as P

precise = lax.Precision.HIGHEST


def solve_blocks(moment, target):
    factor = jnp.linalg.cholesky(moment)
    return jax.vmap(lambda lower, right: jax.scipy.linalg.cho_solve((lower, True), right))(
        factor, target
    )


def shards(ensemble, obs_values, obs_sigma, obs_operator, block_cols, batch_order):
    block_size = obs_operator.shape[-1]
    row_count, mem_dev = ensemble.shape
    nblocks = row_count // block_size
    members = mem_dev * lax.axis_size("mem")
    batches, obs_blocks, col_count = block_cols.shape
    temper = 1.0 / math.sqrt(batches * obs_blocks * block_size)
    offset = lax.axis_index("st") * nblocks
    states = ensemble.reshape(nblocks, block_size, mem_dev)
    eye = jnp.eye(block_size, dtype=jnp.float32)
    slots = jnp.arange(nblocks, dtype=jnp.int32)
    loglik = jnp.zeros((mem_dev,), jnp.float32)
    for batch_step in range(batches):
        chosen = batch_order[batch_step]
        operator_now = lax.dynamic_index_in_dim(obs_operator, chosen, 0, keepdims=False)
        columns = lax.dynamic_index_in_dim(block_cols, chosen, 0, keepdims=False)
        values_now = lax.dynamic_index_in_dim(obs_values, chosen, 0, keepdims=False)
        sigma_now = lax.dynamic_index_in_dim(obs_sigma, chosen, 0, keepdims=False)
        local_ids = columns.reshape(-1) - offset
        selector = (local_ids[:, None] == slots[None, :]).astype(jnp.float32)
        picked = jnp.einsum("ps,sim->pim", selector, states, precision=precise)
        picked = picked.reshape(obs_blocks, col_count, block_size, mem_dev)
        partial_value = jnp.einsum("bkij,bkjm->bim", operator_now, picked, precision=precise)
        image = lax.psum(partial_value, "st")
        misfit = (values_now[:, :, None] - image) / sigma_now[:, :, None]
        loglik = loglik - 0.5 * temper * jnp.sum(misfit * misfit, axis=(0, 1))
        center = lax.psum(jnp.sum(image, axis=2), "mem") / members
        anomaly = image - center[:, :, None]
        moment_sum, cross_sum = lax.psum(
            (
                jnp.einsum("bim,bjm->bij", anomaly, anomaly, precision=precise),
                jnp.einsum("bkim,bjm->bkij", picked, anomaly, precision=precise),
            ),
            "mem",
        )
        moment = moment_sum / (members - 1) + eye * (sigma_now * sigma_now)[:, :, None]
        cross = cross_sum / (members - 1)
        target = (values_now - center)[:, :, None] - 0.5 * anomaly
        weights = solve_blocks(moment, target)
        change = jnp.einsum("bkij,bjm->bkim", cross, weights, precision=precise)
        change = change.reshape(obs_blocks * col_count, block_size, mem_dev)
        states = states + jnp.einsum("ps,pim->sim", selector, change, precision=precise)
    largest_local = jnp.max(loglik)
    largest = lax.pmax(largest_local, "mem")
    scaled = jnp.exp(loglik - largest)
    summed, squares = lax.psum((jnp.sum(scaled), jnp.sum(scaled * scaled)), "mem")
    log_weights = loglik - largest - jnp.log(summed)
    ess = summed * summed / squares
    return (states.reshape(row_count, mem_dev), log_weights, ess)


def solution(mesh):
    placed = (P("st", "mem"), P(), P(), P(), P(), P())
    return jax.shard_map(
        shards,
        mesh=mesh,
        in_specs=placed,
        out_specs=(P("st", "mem"), P("mem"), P()),
        check_vma=False,
    )
```

profile of v0, /device:TPU:0, one launch (start us, length us, event | category | flops | bytes accessed | tf_op | source)
XLA Modules:
  0.0 1220.0 jit_solution(10032874839914542183)
XLA Ops:
  7.2 1.5 fusion.151
  14.0 1.0 copy.121
  17.6 0.7 fusion.133
  18.7 3.1 convolution_bitcast_fusion.7
  21.8 0.7 dynamic-slice_bitcast_fusion
  22.6 0.7 fusion.146
  23.3 35.7 %all-reduce.14.cloned.1.call-done = f32[8,128,32]{1,2,0:T(8,128)} async-done(((f32[8,128,32]{1,2,0:T(8,128)}), f32[8,128,32]{1,2,0:T(8,128)}) %all-reduce.14.cloned.1.call-update) | async-done | bytes 131088 | tf_op jit(solution)/shard_map/psum | solution.py:40
  59.0 1.0 multiply_reduce_fusion.3
  60.1 11.8 psum.127
  71.9 3.9 fusion.50
  75.8 2.9 fusion.77
  79.3 57.4 %all-reduce.28.cloned.1.call-done = (f32[8,128,128]{1,2,0:T(8,128)}, f32[8,2,128,128]{3,2,1,0:T(8,128)}) async-done(((f32[8,128,128]{1,2,0:T(8,128)}, f32[8,2,128,128]{3,2,1,0:T(8,128)}), (f32[8,128,128]{1,2,0:T(8,128)}, f32[8,2,128,128]{3,2,1,0:T(8,128)})) %all-reduce.28.cloned.1.call-update) | async-done | bytes 1572880 | tf_op jit(solution)/shard_map/psum | solution.py:45
  136.7 1.2 multiply_add_fusion.3
  138.1 1.1 fusion.31
  139.2 93.8 %custom-call.14 = f32[8,128,128]{2,1,0:T(8,128)S(1)} custom-call(f32[8,128,128]{2,1,0:T(8,128)S(1)} %fusion.31), custom_call_target="Cholesky" | custom-call | tf_op jit(solution)/shard_map/jit(cholesky)/cholesky | solution.py:11
  233.3 78.6 %custom-call.15 = f32[8,1,128,128]{2,3,1,0:T(8,128)S(1)} custom-call(f32[8,1,128,128]{3,2,1,0:T(8,128)S(1)} %select_bitcast_fusion.3), custom_call_target="InvertDiagBlocksLowerTriangular" | custom-call | tf_op jit(solution)/shard_map/vmap(jit(_cho_solve))/triangular_solve | solution.py:12
  311.9 0.6 fusion.29
  312.5 0.9 convolution_bitcast_fusion.3
  313.4 1.2 fusion.13
  315.3 3.1 convolution_bitcast_fusion.6
  318.5 33.9 %all-reduce.16.cloned.1.call-done = f32[8,128,32]{1,2,0:T(8,128)} async-done(((f32[8,128,32]{1,2,0:T(8,128)}), f32[8,128,32]{1,2,0:T(8,128)}) %all-reduce.16.cloned.1.call-update) | async-done | bytes 131088 | tf_op jit(solution)/shard_map/psum | solution.py:40
  352.4 1.0 multiply_reduce_fusion.2
  353.4 12.0 psum.131
  365.4 3.9 fusion.47
  369.3 2.9 fusion.73
  372.4 57.8 %all-reduce.26.cloned.1.call-done = (f32[8,128,128]{1,2,0:T(8,128)}, f32[8,2,128,128]{3,2,1,0:T(8,128)}) async-done(((f32[8,128,128]{1,2,0:T(8,128)}, f32[8,2,128,128]{3,2,1,0:T(8,128)}), (f32[8,128,128]{1,2,0:T(8,128)}, f32[8,2,128,128]{3,2,1,0:T(8,128)})) %all-reduce.26.cloned.1.call-update) | async-done | bytes 1572880 | tf_op jit(solution)/shard_map/psum | solution.py:45
  430.2 1.2 multiply_add_fusion.2
  431.6 1.1 fusion.27
  432.8 93.8 %custom-call.16 = f32[8,128,128]{2,1,0:T(8,128)S(1)} custom-call(f32[8,128,128]{2,1,0:T(8,128)S(1)} %fusion.27), custom_call_target="Cholesky" | custom-call | tf_op jit(solution)/shard_map/jit(cholesky)/cholesky | solution.py:11
  526.9 78.6 %custom-call.17 = f32[8,1,128,128]{2,3,1,0:T(8,128)S(1)} custom-call(f32[8,1,128,128]{3,2,1,0:T(8,128)S(1)} %select_bitcast_fusion.2), custom_call_target="InvertDiagBlocksLowerTriangular" | custom-call | tf_op jit(solution)/shard_map/vmap(jit(_cho_solve))/triangular_solve | solution.py:12
  605.5 0.6 fusion.25
  606.1 0.9 convolution_bitcast_fusion.2
  607.0 1.2 fusion.10
  608.9 3.1 convolution_bitcast_fusion.5
  612.0 33.9 %all-reduce.18.cloned.1.call-done = f32[8,128,32]{1,2,0:T(8,128)} async-done(((f32[8,128,32]{1,2,0:T(8,128)}), f32[8,128,32]{1,2,0:T(8,128)}) %all-reduce.18.cloned.1.call-update) | async-done | bytes 131088 | tf_op jit(solution)/shard_map/psum | solution.py:40
  645.9 1.0 multiply_reduce_fusion.1
  647.0 12.2 %psum.135 = f32[8,128]{1,0:T(8,128)S(1)} all-reduce(f32[8,128]{1,0:T(8,128)S(1)} %get-tuple-element.10), channel_id=1, replica_groups=mesh['mem'=8,'st'=4] {'mem'}, use_global_device_ids=true, to_apply=%region_14.17 | all-reduce | flops 1024 | bytes 8192 | tf_op jit(solution)/shard_map/psum | solution.py:43
  659.2 3.9 fusion.44
  663.1 2.9 fusion.69
  666.2 57.8 %all-reduce.24.cloned.1.call-done = (f32[8,128,128]{1,2,0:T(8,128)}, f32[8,2,128,128]{3,2,1,0:T(8,128)}) async-done(((f32[8,128,128]{1,2,0:T(8,128)}, f32[8,2,128,128]{3,2,1,0:T(8,128)}), (f32[8,128,128]{1,2,0:T(8,128)}, f32[8,2,128,128]{3,2,1,0:T(8,128)})) %all-reduce.24.cloned.1.call-update) | async-done | bytes 1572880 | tf_op jit(solution)/shard_map/psum | solution.py:45
  724.0 1.2 multiply_add_fusion.1
  725.4 1.1 fusion.23
  726.5 93.8 %custom-call.18 = f32[8,128,128]{2,1,0:T(8,128)S(1)} custom-call(f32[8,128,128]{2,1,0:T(8,128)S(1)} %fusion.23), custom_call_target="Cholesky" | custom-call | tf_op jit(solution)/shard_map/jit(cholesky)/cholesky | solution.py:11
  820.6 78.6 %custom-call.19 = f32[8,1,128,128]{2,3,1,0:T(8,128)S(1)} custom-call(f32[8,1,128,128]{3,2,1,0:T(8,128)S(1)} %select_bitcast_fusion.1), custom_call_target="InvertDiagBlocksLowerTriangular" | custom-call | tf_op jit(solution)/shard_map/vmap(jit(_cho_solve))/triangular_solve | solution.py:12
  899.8 0.9 convolution_bitcast_fusion.1
  900.7 1.2 fusion.7
  902.6 3.1 convolution_bitcast_fusion.4
  905.8 33.9 %all-reduce.20.cloned.1.call-done = f32[8,128,32]{1,2,0:T(8,128)} async-done(((f32[8,128,32]{1,2,0:T(8,128)}), f32[8,128,32]{1,2,0:T(8,128)}) %all-reduce.20.cloned.1.call-update) | async-done | bytes 131088 | tf_op jit(solution)/shard_map/psum | solution.py:40
  939.7 1.0 multiply_reduce_fusion
  940.7 0.6 fusion.147
  941.3 12.4 %pmax.7 = f32[]{:T(128)} all-reduce(f32[]{:T(128)} %get-tuple-element.28), channel_id=1, replica_groups=mesh['mem'=8,'st'=4] {'mem'}, use_global_device_ids=true, to_apply=%region_27.30 | all-reduce | flops 1 | bytes 8 | tf_op jit(solution)/shard_map/pmax | solution.py:60
  953.7 1.3 multiply_reduce_fusion.4
  955.0 12.8 %all-reduce = (f32[8,128]{1,0:T(8,128)S(1)}, f32[]{:T(128)}, f32[]{:T(128)}) all-reduce(f32[8,128]{1,0:T(8,128)S(1)} %get-tuple-element.12, f32[]{:T(128)} %get-tuple-element.14, f32[]{:T(128)} %get-tuple-element.13), channel_id=1, replica_groups=mesh['mem'=8,'st'=4] {'mem'}, use_global_device_ids=true, to_apply=%region_19.22 | all-reduce | flops 1026 | bytes 8208 | tf_op jit(solution)/shard_map/psum | solution.py:43
  967.8 3.9 fusion.41
  971.7 2.9 fusion.65
  977.3 1.2 broadcast_subtract_fusion
  978.4 54.3 %all-reduce.22.cloned.1.call-done = (f32[8,128,128]{1,2,0:T(8,128)}, f32[8,2,128,128]{3,2,1,0:T(8,128)}) async-done(((f32[8,128,128]{1,2,0:T(8,128)}, f32[8,2,128,128]{3,2,1,0:T(8,128)}), (f32[8,128,128]{1,2,0:T(8,128)}, f32[8,2,128,128]{3,2,1,0:T(8,128)})) %all-reduce.22.cloned.1.call-update) | async-done | bytes 1572880 | tf_op jit(solution)/shard_map/psum | solution.py:45
  1032.7 1.2 multiply_add_fusion
  1034.1 1.1 fusion.19
  1035.2 93.8 %custom-call.20 = f32[8,128,128]{2,1,0:T(8,128)S(1)} custom-call(f32[8,128,128]{2,1,0:T(8,128)S(1)} %fusion.19), custom_call_target="Cholesky" | custom-call | tf_op jit(solution)/shard_map/jit(cholesky)/cholesky | solution.py:11
  1129.3 78.6 %custom-call.21 = f32[8,1,128,128]{2,3,1,0:T(8,128)S(1)} custom-call(f32[8,1,128,128]{3,2,1,0:T(8,128)S(1)} %select_bitcast_fusion), custom_call_target="InvertDiagBlocksLowerTriangular" | custom-call | tf_op jit(solution)/shard_map/vmap(jit(_cho_solve))/triangular_solve | solution.py:12
  1208.5 0.9 convolution_bitcast_fusion
  1209.4 1.2 fusion.4
  1211.0 0.8 copy.149
  (73 shorter events, 7.4 us)
Async XLA Ops:
  7.2 51.9 %all-reduce.14.cloned.1.call-start = ((), (), s32[]{:S(2)}) async-start(), calls=%async_computation | async-start | bytes 262144 | tf_op jit(solution)/shard_map/psum | solution.py:40
  21.8 114.9 %all-reduce.28.cloned.1.call-start = ((), (), s32[]{:S(2)}) async-start(), calls=%async_computation.7 | async-start | bytes 3145728 | tf_op jit(solution)/shard_map/psum | solution.py:45
  75.8 236.1 %copy-start.1 = (f32[8,128,32]{1,2,0:T(8,128)S(1)}, f32[8,128,32]{1,2,0:T(8,128)}, u32[]{:S(2)}) copy-start(f32[8,128,32]{1,2,0:T(8,128)} %all-reduce.14.cloned.1.call-done) | copy-start | bytes 393220
  78.7 273.7 %all-reduce.16.cloned.1.call-start = ((), (), s32[]{:S(2)}) async-start(), calls=%async_computation.1 | async-start | bytes 262144 | tf_op jit(solution)/shard_map/psum | solution.py:40
  136.7 176.7 %copy-start.5 = (f32[8,2,128,128]{3,2,1,0:T(8,128)S(1)}, f32[8,2,128,128]{3,2,1,0:T(8,128)}, u32[]{:S(2)}) copy-start(f32[8,2,128,128]{3,2,1,0:T(8,128)} %get-tuple-element.25) | copy-start | bytes 3145732
  318.5 111.8 %all-reduce.26.cloned.1.call-start = ((), (), s32[]{:S(2)}) async-start(), calls=%async_computation.6 | async-start | bytes 3145728 | tf_op jit(solution)/shard_map/psum | solution.py:45
  369.3 236.1 %copy-start.3 = (f32[8,128,32]{1,2,0:T(8,128)S(1)}, f32[8,128,32]{1,2,0:T(8,128)}, u32[]{:S(2)}) copy-start(f32[8,128,32]{1,2,0:T(8,128)} %all-reduce.16.cloned.1.call-done) | copy-start | bytes 393220
  372.2 273.7 %all-reduce.18.cloned.1.call-start = ((), (), s32[]{:S(2)}) async-start(), calls=%async_computation.2 | async-start | bytes 262144 | tf_op jit(solution)/shard_map/psum | solution.py:40
  430.2 176.7 %copy-start.7 = (f32[8,2,128,128]{3,2,1,0:T(8,128)S(1)}, f32[8,2,128,128]{3,2,1,0:T(8,128)}, u32[]{:S(2)}) copy-start(f32[8,2,128,128]{3,2,1,0:T(8,128)} %get-tuple-element.23) | copy-start | bytes 3145732
  612.0 112.0 %all-reduce.24.cloned.1.call-start = ((), (), s32[]{:S(2)}) async-start(), calls=%async_computation.5 | async-start | bytes 3145728 | tf_op jit(solution)/shard_map/psum | solution.py:45
  663.1 236.1 %copy-start.2 = (f32[8,128,32]{1,2,0:T(8,128)S(1)}, f32[8,128,32]{1,2,0:T(8,128)}, u32[]{:S(2)}) copy-start(f32[8,128,32]{1,2,0:T(8,128)} %all-reduce.18.cloned.1.call-done) | copy-start | bytes 393220
  666.0 273.7 %all-reduce.20.cloned.1.call-start = ((), (), s32[]{:S(2)}) async-start(), calls=%async_computation.3 | async-start | bytes 262144 | tf_op jit(solution)/shard_map/psum | solution.py:40
  724.0 176.7 %copy-start.6 = (f32[8,2,128,128]{3,2,1,0:T(8,128)S(1)}, f32[8,2,128,128]{3,2,1,0:T(8,128)}, u32[]{:S(2)}) copy-start(f32[8,2,128,128]{3,2,1,0:T(8,128)} %get-tuple-element.21) | copy-start | bytes 3145732
  905.7 127.0 %all-reduce.22.cloned.1.call-start = ((), (), s32[]{:S(2)}) async-start(), calls=%async_computation.4 | async-start | bytes 3145728 | tf_op jit(solution)/shard_map/psum | solution.py:45
  971.7 236.2 %copy-start = (f32[8,128,32]{1,2,0:T(8,128)S(1)}, f32[8,128,32]{1,2,0:T(8,128)}, u32[]{:S(2)}) copy-start(f32[8,128,32]{1,2,0:T(8,128)} %all-reduce.20.cloned.1.call-done) | copy-start | bytes 393220
  1032.7 176.7 %copy-start.4 = (f32[8,2,128,128]{3,2,1,0:T(8,128)S(1)}, f32[8,2,128,128]{3,2,1,0:T(8,128)}, u32[]{:S(2)}) copy-start(f32[8,2,128,128]{3,2,1,0:T(8,128)} %get-tuple-element.19) | copy-start | bytes 3145732
Sparse Core Ops, SparseCore 0:
  21.9 37.1 all-reduce.13
  78.8 57.8 all-reduce.27
  318.6 33.7 all-reduce.15
  372.3 57.8 all-reduce.25
  612.1 33.7 all-reduce.17
  666.1 57.8 all-reduce.23
  905.9 33.7 all-reduce.19
  974.7 57.9 all-reduce.21
where the time goes:
time: 1220 us
  other arithmetic  709 us (58%)
  waiting for transfers between devices  365 us (30%)
  blocking collectives  61.3 us (5%)
  matrix products  52.9 us (4%)
  between operations  26.4 us (2%)
    another operation x13, other arithmetic, solve_blocks(): factor = jnp.linalg.cholesky(moment)  376 us
    another operation x9, other arithmetic, solve_blocks(): jax.scipy.linalg.cho_solve((lower, True), right)  315 us
    psum x4, waiting for transfers between devices, shards(): lax.psum((jnp.einsum('bim,bjm->bij', anomaly, anomaly, precision=precise)...  227 us
    psum x4, waiting for transfers between devices, shards(): image = lax.psum(partial_value, 'st')  137 us
    psum x4, blocking collectives, shards(): center = lax.psum(jnp.sum(image, axis=2), 'mem') / members  48.9 us
  transfers between devices with their start and end apart: 8, of which 8 were waited for; matrix products, arithmetic and copies ran while one was open for 0% of the time, Pallas kernels for 0%

commit v1 on v0

--- a/solution.py
+++ b/solution.py
@@ -5,6 +5,14 @@
 from jax.sharding import PartitionSpec as P
 
 precise = lax.Precision.HIGHEST
+
+
+def doubling_sum(x, mesh_axis):
+    size, result = (lax.axis_size(mesh_axis), x)
+    for far in [1 << k for k in range(size.bit_length() - 1)]:
+        swap = [(i, i ^ far) for i in range(size)]
+        result = result + lax.ppermute(result, mesh_axis, swap)
+    return result
 
 
 def solve_blocks(moment, target):
@@ -37,7 +45,7 @@
         picked = jnp.einsum("ps,sim->pim", selector, states, precision=precise)
         picked = picked.reshape(obs_blocks, col_count, block_size, mem_dev)
         partial_value = jnp.einsum("bkij,bkjm->bim", operator_now, picked, precision=precise)
-        image = lax.psum(partial_value, "st")
+        image = doubling_sum(partial_value, "st")
         misfit = (values_now[:, :, None] - image) / sigma_now[:, :, None]
         loglik = loglik - 0.5 * temper * jnp.sum(misfit * misfit, axis=(0, 1))
         center = lax.psum(jnp.sum(image, axis=2), "mem") / members

time: 1220 us -> 1130 us (0.926)
  waiting for transfers between devices: 365 us -> 262 us
  starting transfers between devices: 0.5 us -> 19 us
    psum x4 -> x0, waiting for transfers between devices: 137 us -> none  [shards(): image = lax.psum(partial_value, 'st')]
    ppermute x0 -> x8, waiting for transfers between devices: none -> 32 us  [doubling_sum(): result = result + lax.ppermute(result, mesh_axis, swap)]
    ppermute x0 -> x8, starting transfers between devices: none -> 18.7 us  [doubling_sum(): result = result + lax.ppermute(result, mesh_axis, swap)]
  transfers between devices with their start and end apart: 8 -> 12, of which waited for: 8 -> 12; matrix products, arithmetic and copies ran while one was open for 0% -> 0% of each run, Pallas kernels for 0% -> 0%
where the time goes in v1:
time: 1130 us; the launch traced here: 1120 us
  other arithmetic  705 us (62%)
  waiting for transfers between devices  262 us (23%)
  blocking collectives  61.4 us (5%)
  matrix products  42.4 us (4%)
  between operations  26 us (2%)
  starting transfers between devices  19 us (2%)
    another operation x13, other arithmetic, solve_blocks(): factor = jnp.linalg.cholesky(moment)  376 us
    another operation x9, other arithmetic, solve_blocks(): jax.scipy.linalg.cho_solve((lower, True), right)  315 us
    psum x4, waiting for transfers between devices, shards(): lax.psum((jnp.einsum('bim,bjm->bij', anomaly, anomaly, precision=precise)...  230 us
    psum x4, blocking collectives, shards(): center = lax.psum(jnp.sum(image, axis=2), 'mem') / members  49 us
    ppermute x8, waiting for transfers between devices, doubling_sum(): result = result + lax.ppermute(result, mesh_axis, swap)  32 us
  transfers between devices with their start and end apart: 12, of which 12 were waited for; matrix products, arithmetic and copies ran while one was open for 0% of the time, Pallas kernels for 0%

profile of v1, /device:TPU:0, one launch (start us, length us, event | category | flops | bytes accessed | tf_op | source)
XLA Modules:
  0.0 1121.6 jit_solution(15546224544905558509)
XLA Ops:
  7.2 1.5 fusion.151
  14.0 1.0 copy.121
  18.7 2.4 convolution_bitcast_fusion.7
  21.1 3.1 collective-permute-start
  24.2 3.5 collective-permute-done
  27.7 2.8 collective-permute-start.1
  32.0 4.2 collective-permute-done.1
  36.3 11.8 %psum.98 = f32[8,128]{1,0:T(8,128)S(1)} all-reduce(f32[8,128]{1,0:T(8,128)S(1)} %get-tuple-element.6), channel_id=1, replica_groups=mesh['mem'=8,'st'=4] {'mem'}, use_global_device_ids=true, to_apply=%region_1.2 | all-reduce | flops 1024 | bytes 8192 | tf_op jit(solution)/shard_map/psum | solution.py:51
  48.1 3.0 fusion.50
  51.1 1.8 fusion.77
  53.5 59.1 %all-reduce.16.cloned.1.call-done = (f32[8,128,128]{1,2,0:T(8,128)}, f32[8,2,128,128]{3,2,1,0:T(8,128)}) async-done(((f32[8,128,128]{1,2,0:T(8,128)}, f32[8,2,128,128]{3,2,1,0:T(8,128)}), (f32[8,128,128]{1,2,0:T(8,128)}, f32[8,2,128,128]{3,2,1,0:T(8,128)})) %all-reduce.16.cloned.1.call-update) | async-done | bytes 1572880 | tf_op jit(solution)/shard_map/psum | solution.py:53
  112.6 1.2 multiply_add_fusion.3
  114.0 1.1 fusion.31
  115.1 93.8 %custom-call.14 = f32[8,128,128]{2,1,0:T(8,128)S(1)} custom-call(f32[8,128,128]{2,1,0:T(8,128)S(1)} %fusion.31), custom_call_target="Cholesky" | custom-call | tf_op jit(solution)/shard_map/jit(cholesky)/cholesky | solution.py:19
  209.2 78.6 %custom-call.15 = f32[8,1,128,128]{2,3,1,0:T(8,128)S(1)} custom-call(f32[8,1,128,128]{3,2,1,0:T(8,128)S(1)} %select_bitcast_fusion.3), custom_call_target="InvertDiagBlocksLowerTriangular" | custom-call | tf_op jit(solution)/shard_map/vmap(jit(_cho_solve))/triangular_solve | solution.py:20
  288.4 0.9 convolution_bitcast_fusion.3
  289.3 1.2 fusion.13
  291.2 2.4 convolution_bitcast_fusion.6
  293.7 1.7 collective-permute-start.2
  295.4 3.4 collective-permute-done.2
  298.7 2.6 collective-permute-start.3
  301.3 4.7 collective-permute-done.3
  306.2 12.0 %psum.101 = f32[8,128]{1,0:T(8,128)S(1)} all-reduce(f32[8,128]{1,0:T(8,128)S(1)} %get-tuple-element.8), channel_id=1, replica_groups=mesh['mem'=8,'st'=4] {'mem'}, use_global_device_ids=true, to_apply=%region_7.10 | all-reduce | flops 1024 | bytes 8192 | tf_op jit(solution)/shard_map/psum | solution.py:51
  318.3 3.0 fusion.47
  321.3 1.8 fusion.73
  323.3 58.2 %all-reduce.14.cloned.1.call-done = (f32[8,128,128]{1,2,0:T(8,128)}, f32[8,2,128,128]{3,2,1,0:T(8,128)}) async-done(((f32[8,128,128]{1,2,0:T(8,128)}, f32[8,2,128,128]{3,2,1,0:T(8,128)}), (f32[8,128,128]{1,2,0:T(8,128)}, f32[8,2,128,128]{3,2,1,0:T(8,128)})) %all-reduce.14.cloned.1.call-update) | async-done | bytes 1572880 | tf_op jit(solution)/shard_map/psum | solution.py:53
  381.5 1.2 multiply_add_fusion.2
  382.9 1.1 fusion.27
  384.0 93.8 %custom-call.16 = f32[8,128,128]{2,1,0:T(8,128)S(1)} custom-call(f32[8,128,128]{2,1,0:T(8,128)S(1)} %fusion.27), custom_call_target="Cholesky" | custom-call | tf_op jit(solution)/shard_map/jit(cholesky)/cholesky | solution.py:19
  478.1 78.6 %custom-call.17 = f32[8,1,128,128]{2,3,1,0:T(8,128)S(1)} custom-call(f32[8,1,128,128]{3,2,1,0:T(8,128)S(1)} %select_bitcast_fusion.2), custom_call_target="InvertDiagBlocksLowerTriangular" | custom-call | tf_op jit(solution)/shard_map/vmap(jit(_cho_solve))/triangular_solve | solution.py:20
  557.3 0.9 convolution_bitcast_fusion.2
  558.2 1.2 fusion.10
  560.1 2.4 convolution_bitcast_fusion.5
  562.5 1.7 collective-permute-start.4
  564.2 3.4 collective-permute-done.4
  567.6 2.6 collective-permute-start.5
  570.2 4.7 collective-permute-done.5
  575.1 12.3 %psum.104 = f32[8,128]{1,0:T(8,128)S(1)} all-reduce(f32[8,128]{1,0:T(8,128)S(1)} %get-tuple-element.10), channel_id=1, replica_groups=mesh['mem'=8,'st'=4] {'mem'}, use_global_device_ids=true, to_apply=%region_11.14 | all-reduce | flops 1024 | bytes 8192 | tf_op jit(solution)/shard_map/psum | solution.py:51
  587.4 3.0 fusion.44
  590.4 1.8 fusion.69
  592.4 58.2 %all-reduce.12.cloned.1.call-done = (f32[8,128,128]{1,2,0:T(8,128)}, f32[8,2,128,128]{3,2,1,0:T(8,128)}) async-done(((f32[8,128,128]{1,2,0:T(8,128)}, f32[8,2,128,128]{3,2,1,0:T(8,128)}), (f32[8,128,128]{1,2,0:T(8,128)}, f32[8,2,128,128]{3,2,1,0:T(8,128)})) %all-reduce.12.cloned.1.call-update) | async-done | bytes 1572880 | tf_op jit(solution)/shard_map/psum | solution.py:53
  650.6 1.2 multiply_add_fusion.1
  652.0 1.1 fusion.23
  653.1 93.8 %custom-call.18 = f32[8,128,128]{2,1,0:T(8,128)S(1)} custom-call(f32[8,128,128]{2,1,0:T(8,128)S(1)} %fusion.23), custom_call_target="Cholesky" | custom-call | tf_op jit(solution)/shard_map/jit(cholesky)/cholesky | solution.py:19
  747.2 78.6 %custom-call.19 = f32[8,1,128,128]{2,3,1,0:T(8,128)S(1)} custom-call(f32[8,1,128,128]{3,2,1,0:T(8,128)S(1)} %select_bitcast_fusion.1), custom_call_target="InvertDiagBlocksLowerTriangular" | custom-call | tf_op jit(solution)/shard_map/vmap(jit(_cho_solve))/triangular_solve | solution.py:20
  826.4 0.9 convolution_bitcast_fusion.1
  827.3 1.2 fusion.7
  829.2 2.4 convolution_bitcast_fusion.4
  831.7 1.7 collective-permute-start.6
  833.3 3.4 collective-permute-done.6
  836.7 2.6 collective-permute-start.7
  839.3 4.7 collective-permute-done.7
  844.8 12.4 %pmax.7 = f32[]{:T(128)} all-reduce(f32[]{:T(128)} %get-tuple-element.28), channel_id=1, replica_groups=mesh['mem'=8,'st'=4] {'mem'}, use_global_device_ids=true, to_apply=%region_23.26 | all-reduce | flops 1 | bytes 8 | tf_op jit(solution)/shard_map/pmax | solution.py:68
  857.2 1.3 multiply_reduce_fusion.4
  858.5 12.9 %all-reduce = (f32[8,128]{1,0:T(8,128)S(1)}, f32[]{:T(128)}, f32[]{:T(128)}) all-reduce(f32[8,128]{1,0:T(8,128)S(1)} %get-tuple-element.12, f32[]{:T(128)} %get-tuple-element.14, f32[]{:T(128)} %get-tuple-element.13), channel_id=1, replica_groups=mesh['mem'=8,'st'=4] {'mem'}, use_global_device_ids=true, to_apply=%region_15.18 | all-reduce | flops 1026 | bytes 8208 | tf_op jit(solution)/shard_map/psum | solution.py:51
  871.4 3.0 fusion.41
  874.4 1.8 fusion.65
  878.9 1.2 broadcast_subtract_fusion
  880.0 54.6 %all-reduce.10.cloned.1.call-done = (f32[8,128,128]{1,2,0:T(8,128)}, f32[8,2,128,128]{3,2,1,0:T(8,128)}) async-done(((f32[8,128,128]{1,2,0:T(8,128)}, f32[8,2,128,128]{3,2,1,0:T(8,128)}), (f32[8,128,128]{1,2,0:T(8,128)}, f32[8,2,128,128]{3,2,1,0:T(8,128)})) %all-reduce.10.cloned.1.call-update) | async-done | bytes 1572880 | tf_op jit(solution)/shard_map/psum | solution.py:53
  934.6 1.2 multiply_add_fusion
  936.0 1.1 fusion.19
  937.1 93.8 %custom-call.20 = f32[8,128,128]{2,1,0:T(8,128)S(1)} custom-call(f32[8,128,128]{2,1,0:T(8,128)S(1)} %fusion.19), custom_call_target="Cholesky" | custom-call | tf_op jit(solution)/shard_map/jit(cholesky)/cholesky | solution.py:19
  1031.2 78.6 %custom-call.21 = f32[8,1,128,128]{2,3,1,0:T(8,128)S(1)} custom-call(f32[8,1,128,128]{3,2,1,0:T(8,128)S(1)} %select_bitcast_fusion), custom_call_target="InvertDiagBlocksLowerTriangular" | custom-call | tf_op jit(solution)/shard_map/vmap(jit(_cho_solve))/triangular_solve | solution.py:20
  1111.3 1.2 fusion.4
  (73 shorter events, 13.5 us)
Async XLA Ops:
  7.2 105.4 %all-reduce.16.cloned.1.call-start = ((), (), s32[]{:S(2)}) async-start(), calls=%async_computation.3 | async-start | bytes 3145728 | tf_op jit(solution)/shard_map/psum | solution.py:53
  21.1 6.6 collective-permute-start
  27.7 8.5 collective-permute-start.1
  52.9 328.6 %all-reduce.14.cloned.1.call-start = ((), (), s32[]{:S(2)}) async-start(), calls=%async_computation.2 | async-start | bytes 3145728 | tf_op jit(solution)/shard_map/psum | solution.py:53
  112.6 176.7 %copy-start.1 = (f32[8,2,128,128]{3,2,1,0:T(8,128)S(1)}, f32[8,2,128,128]{3,2,1,0:T(8,128)}, u32[]{:S(2)}) copy-start(f32[8,2,128,128]{3,2,1,0:T(8,128)} %get-tuple-element.25) | copy-start | bytes 3145732
  293.7 5.0 collective-permute-start.2
  298.7 7.3 collective-permute-start.3
  323.1 327.5 %all-reduce.12.cloned.1.call-start = ((), (), s32[]{:S(2)}) async-start(), calls=%async_computation.1 | async-start | bytes 3145728 | tf_op jit(solution)/shard_map/psum | solution.py:53
  381.5 176.7 %copy-start.3 = (f32[8,2,128,128]{3,2,1,0:T(8,128)S(1)}, f32[8,2,128,128]{3,2,1,0:T(8,128)}, u32[]{:S(2)}) copy-start(f32[8,2,128,128]{3,2,1,0:T(8,128)} %get-tuple-element.23) | copy-start | bytes 3145732
  562.5 5.0 collective-permute-start.4
  567.6 7.3 collective-permute-start.5
  592.2 342.4 %all-reduce.10.cloned.1.call-start = ((), (), s32[]{:S(2)}) async-start(), calls=%async_computation | async-start | bytes 3145728 | tf_op jit(solution)/shard_map/psum | solution.py:53
  650.6 176.7 %copy-start.2 = (f32[8,2,128,128]{3,2,1,0:T(8,128)S(1)}, f32[8,2,128,128]{3,2,1,0:T(8,128)}, u32[]{:S(2)}) copy-start(f32[8,2,128,128]{3,2,1,0:T(8,128)} %get-tuple-element.21) | copy-start | bytes 3145732
  831.7 5.0 collective-permute-start.6
  836.7 7.3 collective-permute-start.7
  934.6 176.7 %copy-start = (f32[8,2,128,128]{3,2,1,0:T(8,128)S(1)}, f32[8,2,128,128]{3,2,1,0:T(8,128)}, u32[]{:S(2)}) copy-start(f32[8,2,128,128]{3,2,1,0:T(8,128)} %get-tuple-element.19) | copy-start | bytes 3145732
Sparse Core Ops, SparseCore 0:
  53.0 59.5 all-reduce.15
  323.2 58.2 all-reduce.13
  592.3 58.2 all-reduce.11
  876.3 58.2 all-reduce.9
